TPU v7x, 256 devices: a whole 4x4x8 slice. The times are simulated.
256 devices in a mesh: gz: 64 (over x, y, z_hi, core), gy: 4 (over z_lo).
Axes of the slice: x: 4, y: 4, z: 8 (z_hi: 2, z_lo: 4; z = z_hi * 4 + z_lo), core: 2. Of those that a mesh axis runs over, the one named last changes fastest.
Arguments:
- velocity: float32 [2, 2, 1536, 7680], P(None, None, 'gz', 'gy'), may hold values from -0.15625 to 0.15625
- vorticity: float32 [2, 2, 1536, 7680], P(None, None, 'gz', 'gy'), may hold values from -0.15625 to 0.15625
Outputs:
- criterion: float32 [2, 4, 1920, 1536], P(None, None, 'gz', 'gy')
All inputs are finite; a program needn't handle non-finite values.
Results may differ from a plain program's by a relative error of at most 0.0003.
Values sent between devices are 32-bit elements; how exact they have to be, the bound alone decides.
No kernel may reach another device: no remote copies, remote signals or barrier semaphores. Data moves between devices by JAX's collectives and lax.ppermute only.
A program may use at most 128 MiB of HBM per device.

v0:
```python
import math

import jax
import jax.numpy as jnp
from jax import lax
from jax.sharding import PartitionSpec as P

NY = 1536
NZ = 7680
KX = 2


def cut_along(array, dim, length):
    lengths = array.shape
    tiles = array.reshape(*lengths[:dim], length, lengths[dim] // length, *lengths[dim + 1 :])
    return jnp.moveaxis(tiles, dim, 0)


def piece_ends(length, count):
    unit = 8 if length >= 8 * count else 1
    return [length // unit * k // count * unit for k in range(1, count)]


def laid_out(tiles, dim):
    lengths = list(tiles.shape[1:])
    lengths[dim] *= tiles.shape[0]
    return jnp.moveaxis(tiles, 0, dim).reshape(lengths)


def exchange_in_pieces(array, axis, pieces, split_dim, concat_dim):
    tiles = cut_along(array, split_dim, lax.axis_size(axis))
    widest = max(range(1, max(2, tiles.ndim - 1)), key=lambda d: tiles.shape[d])
    gathered = []
    for piece in jnp.split(tiles, piece_ends(tiles.shape[widest], pieces), axis=widest):
        if piece.size:
            gathered.append(lax.all_to_all(piece, axis, split_axis=0, concat_axis=0, tiled=True))
    return laid_out(jnp.concatenate(gathered, axis=widest), concat_dim)


def cheb_tables(order):
    points = jnp.arange(order, dtype=jnp.int32)
    turns = points[None, :] * (2 * points[:, None] + 1) % (4 * order)
    angle = turns.astype(jnp.float32) * (math.pi / (2 * order))
    degree = points[None, :].astype(jnp.float32)
    return (jnp.cos(angle), -(math.pi / order) * degree * jnp.sin(angle))


def spanwise(index):
    signed = jnp.where(index < NZ // 2, index, index - NZ)
    return signed.astype(jnp.float32) * (2.0 / NZ)


def velocities(wave_x, wave_z, growth, vortex):
    inverse = 1.0 / (wave_x * wave_x + wave_z * wave_z)
    first_re = wave_x * growth[0] - wave_z * vortex[0]
    first_im = wave_x * growth[1] - wave_z * vortex[1]
    second_re = wave_z * growth[0] + wave_x * vortex[0]
    second_im = wave_z * growth[1] + wave_x * vortex[1]
    stream = (-first_im * inverse, first_re * inverse)
    across = (-second_im * inverse, second_re * inverse)
    return (stream, across)


def wall_slope(field):
    widths = [(0, 0)] * (field.ndim - 1) + [(1, 1)]
    padded = jnp.pad(field, widths)
    return 0.5 * (padded[..., 2:] - padded[..., :-2])


def q_value(wave_x, wave_z, normal, growth, stream, across, stream_grad, across_grad):
    total = wave_x * wave_x * (stream[0] * stream[0] + stream[1] * stream[1])
    total = total + growth[0] * growth[0] + growth[1] * growth[1]
    total = total + wave_z * wave_z * (across[0] * across[0] + across[1] * across[1])
    total = total + 2.0 * wave_x * (stream_grad[1] * normal[0] - stream_grad[0] * normal[1])
    total = total + 2.0 * wave_x * wave_z * (stream[0] * across[0] + stream[1] * across[1])
    total = total + 2.0 * wave_z * (normal[0] * across_grad[1] - normal[1] * across_grad[0])
    squares = (
        stream[0] * stream[0]
        + stream[1] * stream[1]
        + normal[0] * normal[0]
        + normal[1] * normal[1]
    )
    squares = squares + across[0] * across[0] + across[1] * across[1]
    gradient = (wave_x * wave_x + wave_z * wave_z) * squares
    gradient = gradient + stream_grad[0] * stream_grad[0] + stream_grad[1] * stream_grad[1]
    gradient = gradient + growth[0] * growth[0] + growth[1] * growth[1]
    gradient = gradient + across_grad[0] * across_grad[0] + across_grad[1] * across_grad[1]
    return 0.25 * (gradient - total)


def local(velocity, vorticity):
    groups = lax.axis_size("gy")
    values, slopes = cheb_tables(NY)
    field_v = lax.all_to_all(velocity, "gz", split_axis=3, concat_axis=2, tiled=True)
    field_o = lax.all_to_all(vorticity, "gz", split_axis=3, concat_axis=2, tiled=True)
    normal = jnp.einsum("cknz,jn->ckzj", field_v, values, precision=lax.Precision.HIGHEST)
    growth = jnp.einsum("cknz,jn->ckzj", field_v, slopes, precision=lax.Precision.HIGHEST)
    vortex = jnp.einsum("cknz,jn->ckzj", field_o, values, precision=lax.Precision.HIGHEST)
    normal, growth, vortex = (normal, growth, vortex)
    modes = normal.shape[1]
    columns = normal.shape[2]
    block = NZ // groups
    wave_base = (jnp.arange(modes, dtype=jnp.int32) + 1).astype(jnp.float32) / KX
    span_index = (
        lax.axis_index("gy") * block
        + lax.axis_index("gz") * columns
        + jnp.arange(columns, dtype=jnp.int32)
    )
    wave_z = spanwise(span_index)[None, :, None]
    wave_x = wave_base[:, None, None]
    stream, across = velocities(wave_x, wave_z, (growth[0], growth[1]), (vortex[0], vortex[1]))
    stream_grad = (wall_slope(stream[0]), wall_slope(stream[1]))
    across_grad = (wall_slope(across[0]), wall_slope(across[1]))
    result = q_value(
        wave_x,
        wave_z,
        (normal[0], normal[1]),
        (growth[0], growth[1]),
        stream,
        across,
        stream_grad,
        across_grad,
    )
    return exchange_in_pieces(result[:, None], "gy", 2, 3, 1)


def solution(mesh):
    placed = (P(None, None, "gz", "gy"), P(None, None, "gz", "gy"))
    return jax.shard_map(
        local, mesh=mesh, in_specs=placed, out_specs=P(None, None, "gz", "gy"), check_vma=False
    )
```

profile of v0, /device:TPU:6, one launch (start us, length us, event | category | flops | bytes accessed | tf_op | source)
XLA Modules:
  0.0 263.3 jit_solution(17485283849762005317)
XLA Ops:
  0.0 5.5 %copy.12 = f32[2,2,24,1920]{2,1,0,3:T(2,128)} copy(f32[2,2,24,1920]{3,2,1,0:T(8,128)} %param.2) | data formatting | bytes 1474560 | tf_op args[0]
  5.5 8.1 %reshape.125 = f32[64,1,2880]{2,1,0:T(1,128)} reshape(f32[1920,2,2,24]{3,2,1,0:T(2,128)} %bitcast.107) | data formatting | bytes 1474560
  13.7 15.4 %all-to-all-start = ((f32[64,1,2880]{2,1,0:T(1,128)}), f32[64,1,2880]{2,1,0:T(1,128)S(1)}, u32[]{:S(2)}, u32[]{:S(2)}) async-start(f32[64,1,2880]{2,1,0:T(1,128)} %reshape.125), calls=%async_computation | async-start | bytes 1507328 | tf_op jit(solution)/shard_map/all_to_all | solution.py:94
  29.2 3.7 %copy.16 = f32[2,2,24,1920]{2,1,0,3:T(2,128)} copy(f32[2,2,24,1920]{3,2,1,0:T(8,128)S(1)} %copy-done) | data formatting | bytes 1474560 | tf_op args[1]
  32.9 8.2 %reshape.123 = f32[64,1,2880]{2,1,0:T(1,128)} reshape(f32[1920,2,2,24]{3,2,1,0:T(2,128)} %bitcast.108) | data formatting | bytes 1474560
  41.1 37.4 %fusion.70 = f32[1536,1536,1,1]{1,0,3,2:T(8,128)} fusion(s32[1536]{0:T(1024)S(1)} %multiply_add_fusion), kind=kLoop, calls=%fused_computation.6.clone.clone.clone | loop fusion | flops 21233664 | bytes 9443328 | tf_op jit(solution)/shard_map/cknz,jn->ckzj/dot_general | solution.py:96
  78.6 0.1 broadcast_add_fusion
  78.6 37.6 %fusion.68 = f32[1536,1536,1,1]{1,0,3,2:T(8,128)} fusion(s32[1536]{0:T(1024)S(1)} %multiply_add_fusion), kind=kLoop, calls=%fused_computation.8.clone.clone.clone.1 | loop fusion | flops 21233664 | bytes 9443328 | tf_op jit(solution)/shard_map/cknz,jn->ckzj/dot_general | solution.py:98
  116.2 13.0 %all-to-all-start.1 = ((f32[64,1,2880]{2,1,0:T(1,128)}), f32[64,1,2880]{2,1,0:T(1,128)S(1)}, u32[]{:S(2)}, u32[]{:S(2)}) async-start(f32[64,1,2880]{2,1,0:T(1,128)} %reshape.123), calls=%async_computation.1 | async-start | bytes 1507328 | tf_op jit(solution)/shard_map/all_to_all | solution.py:95
  129.3 37.6 %fusion.72 = f32[1536,1536,1,1]{1,0,3,2:T(8,128)} fusion(s32[1536]{0:T(1024)S(1)} %multiply_add_fusion, f32[1536]{0:T(1024)S(1)} %convert_multiply_fusion), kind=kLoop, calls=%fused_computation.4.clone.clone.clone.1 | loop fusion | flops 23592960 | bytes 9449472 | tf_op jit(solution)/shard_map/cknz,jn->ckzj/dot_general | solution.py:97
  166.9 0.5 broadcast.221
  167.4 2.4 reduce.1
  169.9 6.9 %reshape.126 = f32[1920,2,2,24]{3,2,1,0:T(2,128)} reshape(f32[64,2880]{1,0:T(8,128)S(1)} %reduce.1) | data formatting | bytes 1474560
  176.7 4.8 %copy.44 = f32[2,2,24,64,30]{2,3,1,4,0:T(8,128)} copy(f32[2,2,24,64,30]{2,1,0,4,3:T(2,128)} %bitcast.103) | data formatting | bytes 1474560 | tf_op jit(solution)/shard_map/all_to_all | solution.py:94
  181.5 4.1 %all_to_all.35 = f32[2,2,1536,30]{2,1,3,0:T(2,128)S(1)} reshape(f32[2,2,64,24,30]{3,2,1,4,0:T(8,128)} %bitcast.104) | data formatting | bytes 1474560 | tf_op jit(solution)/shard_map/all_to_all | solution.py:94
  185.6 2.4 reduce
  188.0 7.1 %reshape.124 = f32[1920,2,2,24]{3,2,1,0:T(2,128)} reshape(f32[64,2880]{1,0:T(8,128)S(1)} %reduce) | data formatting | bytes 1474560
  195.1 4.8 %copy.43 = f32[2,2,24,64,30]{2,3,1,4,0:T(8,128)} copy(f32[2,2,24,64,30]{2,1,0,4,3:T(2,128)} %bitcast.105) | data formatting | bytes 1474560 | tf_op jit(solution)/shard_map/all_to_all | solution.py:95
  199.9 4.1 %all_to_all.39 = f32[2,2,1536,30]{2,1,3,0:T(2,128)S(1)} reshape(f32[2,2,64,24,30]{3,2,1,4,0:T(8,128)} %bitcast.106) | data formatting | bytes 1474560 | tf_op jit(solution)/shard_map/all_to_all | solution.py:95
  204.0 12.4 %fusion.36 = f32[2,2,30,1536]{3,2,1,0:T(8,128)S(1)} fusion(f32[2,2,1536,30]{2,1,3,0:T(2,128)S(1)} %all_to_all.35, f32[1536,1536,1,1]{1,0,3,2:T(8,128)} %fusion.72), kind=kOutput, calls=%fused_computation.30 | convolution fusion | flops 3397386240 | bytes 10911744 | tf_op jit(solution)/shard_map/cknz,jn->ckzj/dot_general | solution.py:97
  216.4 12.6 %fusion.33 = f32[2,2,30,1536]{3,2,1,0:T(8,128)S(1)} fusion(f32[2,2,1536,30]{2,1,3,0:T(2,128)S(1)} %all_to_all.35, f32[1536,1536,1,1]{1,0,3,2:T(8,128)} %fusion.70), kind=kOutput, calls=%fused_computation.29 | convolution fusion | flops 3397386240 | bytes 10911744 | tf_op jit(solution)/shard_map/cknz,jn->ckzj/dot_general | solution.py:96
  229.1 9.9 %fusion.30 = f32[2,2,30,1536]{3,2,1,0:T(8,128)S(1)} fusion(f32[2,2,1536,30]{2,1,3,0:T(2,128)S(1)} %all_to_all.39, f32[1536,1536,1,1]{1,0,3,2:T(8,128)S(1)} %bitcast.102), kind=kOutput, calls=%fused_computation.28 | convolution fusion | flops 3397386240 | bytes 10911744 | tf_op jit(solution)/shard_map/cknz,jn->ckzj/dot_general | solution.py:98
  238.9 0.3 negate_multiply_fusion
  239.3 1.2 subtract_multiply_fusion
  240.5 0.1 reshape.122
  240.7 0.7 copy.22
  241.4 3.3 %all-to-all-start.2 = ((f32[4,2,1,8,384]{4,1,3,2,0:T(2,128)}), f32[4,2,1,8,384]{4,1,3,2,0:T(2,128)S(1)}, u32[]{:S(2)}, u32[]{:S(2)}) async-start(f32[4,2,1,8,384]{4,1,3,2,0:T(2,128)} %copy.22), calls=%async_computation.2 | async-start | bytes 196608 | tf_op jit(solution)/shard_map/all_to_all | solution.py:36
  244.7 0.1 copy.23
  244.9 5.8 %all-to-all-done.2 = f32[4,2,1,8,384]{4,1,3,2,0:T(2,128)S(1)} async-done(((f32[4,2,1,8,384]{4,1,3,2,0:T(2,128)}), f32[4,2,1,8,384]{4,1,3,2,0:T(2,128)S(1)}, u32[]{:S(2)}, u32[]{:S(2)}) %all-to-all-start.2) | async-done | bytes 98336 | tf_op jit(solution)/shard_map/all_to_all | solution.py:36
  250.6 11.2 %all_to_all.46 = f32[4,2,1,22,384]{4,1,3,2,0:T(2,128)S(1)} all-to-all(f32[4,2,1,22,384]{4,1,3,2,0:T(2,128)S(1)} %copy.23), channel_id=1, replica_groups=mesh['gz'=64,'gy'=4] {'gy'}, dimensions={0} | all-to-all | bytes 540672 | tf_op jit(solution)/shard_map/all_to_all | solution.py:36
  261.9 0.2 maximum_bitcast_fusion
  262.0 0.8 copy.24
  (22 shorter events, 0.2 us)
Async XLA Ops:
  0.0 29.2 %copy-start = (f32[2,2,24,1920]{3,2,1,0:T(8,128)S(1)}, f32[2,2,24,1920]{3,2,1,0:T(8,128)}, u32[]{:S(2)}) copy-start(f32[2,2,24,1920]{3,2,1,0:T(8,128)} %param.3) | copy-start | bytes 2211844
  13.7 102.5 %all-to-all-start = ((f32[64,1,2880]{2,1,0:T(1,128)}), f32[64,1,2880]{2,1,0:T(1,128)S(1)}, u32[]{:S(2)}, u32[]{:S(2)}) async-start(f32[64,1,2880]{2,1,0:T(1,128)} %reshape.125), calls=%async_computation | async-start | bytes 1507328 | tf_op jit(solution)/shard_map/all_to_all | solution.py:94
  116.2 69.4 %all-to-all-start.1 = ((f32[64,1,2880]{2,1,0:T(1,128)}), f32[64,1,2880]{2,1,0:T(1,128)S(1)}, u32[]{:S(2)}, u32[]{:S(2)}) async-start(f32[64,1,2880]{2,1,0:T(1,128)} %reshape.123), calls=%async_computation.1 | async-start | bytes 1507328 | tf_op jit(solution)/shard_map/all_to_all | solution.py:95
  204.0 25.0 %slice-start = ((s8[9437184]{0:T(1024)(128)(4,1)}), s8[4194304]{0:T(1024)(128)(4,1)S(1)}, s32[]{:S(2)}) async-start(s8[9437184]{0:T(1024)(128)(4,1)} %bitcast.101), calls=%async_computation.4 | async-start | bytes 8388608
  204.0 25.0 %slice-start.1 = ((s8[9437184]{0:T(1024)(128)(4,1)}), s8[4194304]{0:T(1024)(128)(4,1)S(1)}, s32[]{:S(2)}) async-start(s8[9437184]{0:T(1024)(128)(4,1)} %bitcast.101), calls=%async_computation.5 | async-start | bytes 8388608
  216.4 12.6 %slice-start.2 = ((s8[9437184]{0:T(1024)(128)(4,1)}), s8[1048576]{0:T(1024)(128)(4,1)S(1)}, s32[]{:S(2)}) async-start(s8[9437184]{0:T(1024)(128)(4,1)} %bitcast.101), calls=%async_computation.6 | async-start | bytes 2097152
  241.4 9.3 %all-to-all-start.2 = ((f32[4,2,1,8,384]{4,1,3,2,0:T(2,128)}), f32[4,2,1,8,384]{4,1,3,2,0:T(2,128)S(1)}, u32[]{:S(2)}, u32[]{:S(2)}) async-start(f32[4,2,1,8,384]{4,1,3,2,0:T(2,128)} %copy.22), calls=%async_computation.2 | async-start | bytes 196608 | tf_op jit(solution)/shard_map/all_to_all | solution.py:36
where the time goes:
time: 268 us; the launch traced here: 263 us
  other arithmetic  119 us (44%)
  local copies, waits for them, and re-layouts  59.6 us (22%)
  matrix products  34.8 us (13%)
  starting transfers between devices  31.8 us (12%)
  blocking collectives  11.2 us (4%)
  waiting for transfers between devices  5.77 us (2%)
    unnamed x14, local copies, waits for them, and re-layouts  39.5 us
    dot_general x1, other arithmetic, local(): jnp.einsum('cknz,jn->ckzj', field_v, slopes, precision=lax.Precision.HIGH...  37.6 us
    dot_general x1, other arithmetic, local(): jnp.einsum('cknz,jn->ckzj', field_o, values, precision=lax.Precision.HIGH...  37.6 us
    dot_general x1, other arithmetic, local(): jnp.einsum('cknz,jn->ckzj', field_v, values, precision=lax.Precision.HIGH...  37.4 us
    all_to_all x1, starting transfers between devices, local(): lax.all_to_all(velocity, 'gz', split_axis=3, concat_axis=2, tiled=True)  15.4 us
    all_to_all x1, starting transfers between devices, local(): lax.all_to_all(vorticity, 'gz', split_axis=3, concat_axis=2, tiled=True)  13 us
    dot_general x1, matrix products, local(): jnp.einsum('cknz,jn->ckzj', field_v, values, precision=lax.Precision.HIGH...  12.6 us
    dot_general x1, matrix products, local(): jnp.einsum('cknz,jn->ckzj', field_v, slopes, precision=lax.Precision.HIGH...  12.4 us
  transfers between devices with their start and end apart: 3, of which 1 were waited for; matrix products, arithmetic and copies ran while one was open for 53% of the time, Pallas kernels for 0%

commit v1 on v0

v1 whole, which is shorter than its diff:
```python
import math

import jax
import jax.numpy as jnp
from jax import lax
from jax.experimental import pallas as pl
from jax.experimental.pallas import tpu as pltpu
from jax.sharding import PartitionSpec as P

NY = 1536
NZ = 7680
KX = 2
HALF = NY // 2
SLOT = 32
LANES = 128
GROUPS = ((0,), (1,))
LIMIT = 48 * 1024 * 1024


def spanwise(index):
    signed = jnp.where(index < NZ // 2, index, index - NZ)
    return signed.astype(jnp.float32) * (2.0 / NZ)


def pack_kernel(cols, v_ref, o_ref, out_ref):
    peers, rows, width = out_ref.shape
    lane = lax.broadcasted_iota(jnp.int32, (8, LANES), 1)
    chunks = v_ref.shape[-1] // LANES
    for i in range(width // LANES):
        for t in range(rows // 8):
            at = pl.ds(8 * t, 8)
            for a in range(peers):
                k, off = divmod(cols * a, LANES)
                merged = None
                for g in range(4):
                    ref, c = (v_ref, o_ref)[g // 2], g % 2
                    piece = ref[c, i, at, pl.ds(LANES * k, LANES)]
                    if off + cols > LANES:
                        after = ref[c, i, at, pl.ds(LANES * ((k + 1) % chunks), LANES)]
                        piece = jnp.where(lane >= off, piece, after)
                    shift = (SLOT * g - off) % LANES
                    if shift:
                        piece = pltpu.roll(piece, shift, 1)
                    merged = piece if merged is None else jnp.where(lane >= SLOT * g, piece, merged)
                out_ref[a, at, pl.ds(LANES * i, LANES)] = merged


def pack(velocity, vorticity, modes, peers):
    _, _, rows, span = velocity.shape
    width = LANES * len(modes)
    block = pl.BlockSpec((2, len(modes), rows, span), lambda i: (0, modes[0] // len(modes), 0, 0))
    return pl.pallas_call(
        lambda *refs: pack_kernel(span // peers, *refs),
        grid=(1,),
        in_specs=[block, block],
        out_specs=pl.BlockSpec((peers, rows, width), lambda i: (0, 0, 0)),
        out_shape=jax.ShapeDtypeStruct((peers, rows, width), jnp.float32),
        compiler_params=pltpu.CompilerParams(vmem_limit_bytes=LIMIT),
        name="pack",
    )(velocity, vorticity)


def table_kernel(base_ref, hi_ref, lo_ref):
    c, s = base_ref[0, 0], base_ref[0, 1]
    turn_c, turn_s = base_ref[0, 2], base_ref[0, 3]
    for q in range(HALF // LANES):
        high = c.astype(jnp.bfloat16)
        hi_ref[0, :, pl.ds(LANES * q, LANES)] = high
        lo_ref[0, :, pl.ds(LANES * q, LANES)] = (c - high.astype(jnp.float32)).astype(jnp.bfloat16)
        c, s = c * turn_c - s * turn_s, s * turn_c + c * turn_s


def tables():
    point = jnp.arange(HALF, dtype=jnp.int32)[:, None]
    first = 2 * jnp.arange(LANES, dtype=jnp.int32)[None, :]
    turn = jnp.full((1, LANES), 2 * LANES, jnp.int32)

    def angle(degree):
        return (degree * (2 * point + 1) % (4 * NY)).astype(jnp.float32) * (math.pi / (2 * NY))

    degrees = jnp.stack([angle(first), angle(first + 1)])
    turns = jnp.broadcast_to(angle(turn), degrees.shape)
    base = jnp.stack([jnp.cos(degrees), jnp.sin(degrees), jnp.cos(turns), jnp.sin(turns)], axis=1)
    rows = 64
    shape = jax.ShapeDtypeStruct((2, HALF, HALF), jnp.bfloat16)
    return pl.pallas_call(
        table_kernel,
        grid=(2, HALF // rows),
        in_specs=[pl.BlockSpec((1, 4, rows, LANES), lambda p, i: (p, 0, i, 0))],
        out_specs=[pl.BlockSpec((1, rows, HALF), lambda p, i: (p, i, 0))] * 2,
        out_shape=[shape, shape],
        compiler_params=pltpu.CompilerParams(vmem_limit_bytes=LIMIT),
        name="tables",
    )(base)


def degree_weights():
    degree = jnp.arange(NY, dtype=jnp.int32).reshape(HALF, 2).T.astype(jnp.float32)
    scaled = degree * (math.pi / NY)
    stretch = scaled * jnp.sin(scaled)
    edge = -0.5 * scaled * jnp.sin(0.5 * scaled)
    both = jnp.stack([stretch, edge], axis=1)
    return jnp.broadcast_to(both[..., None], (2, 2, HALF, LANES))


def criterion_kernel(x_ref, hi_ref, lo_ref, weight_ref, wave_ref, flip_ref, out_ref, low_ref, top_ref):
    lane = lax.broadcasted_iota(jnp.int32, (1, LANES), 1)
    normal = lane < 2 * SLOT
    for i in range(x_ref.shape[1] // LANES):
        wave = wave_ref[i][:1]
        halves = []
        for parity in range(2):
            x = x_ref[pl.ds(parity, HALF, stride=2), pl.ds(LANES * i, LANES)]
            scaled = x * jnp.where(normal, wave + weight_ref[parity, 0], 1.0)
            edge = jnp.sum(x * weight_ref[parity, 1], axis=0, keepdims=True)
            high = scaled.astype(jnp.bfloat16)
            low = (scaled - high.astype(jnp.float32)).astype(jnp.bfloat16)
            wide = jnp.concatenate([high, low], axis=1)
            first = jnp.dot(hi_ref[parity], wide, preferred_element_type=jnp.float32)
            second = jnp.dot(lo_ref[parity], high, preferred_element_type=jnp.float32)
            total = first[:, :LANES] + first[:, LANES:] + second
            row = lax.broadcasted_iota(jnp.int32, (HALF, LANES), 0)
            halves.append(total + jnp.where((row == 0) & normal, edge, 0.0))
        low_ref[pl.ds(8, HALF), :] = halves[0] + halves[1]
        top_ref[pl.ds(8, HALF), :] = halves[0] - halves[1]
        outside = jnp.zeros((8, LANES), jnp.float32)
        low_ref[pl.ds(0, 8), :] = outside
        top_ref[pl.ds(0, 8), :] = outside
        low_ref[pl.ds(8 + HALF, 1), :] = top_ref[pl.ds(7 + HALF, 1), :]
        top_ref[pl.ds(8 + HALF, 1), :] = low_ref[pl.ds(7 + HALF, 1), :]
        inverse = 0.25 / wave
        for b in range(HALF // LANES):
            parts = []
            for ref in (low_ref, top_ref):
                here = ref[pl.ds(8 + LANES * b, LANES), :]
                slope = 0.5 * (ref[pl.ds(9 + LANES * b, LANES), :] - ref[pl.ds(7 + LANES * b, LANES), :])
                square = here * here
                parts.append(jnp.where(normal, square * inverse, 0.25 * square + slope * slope * inverse))
            folded = jnp.where(normal, parts[0], parts[1])
            folded = folded + pltpu.roll(jnp.where(normal, parts[1], parts[0]), 2 * SLOT, 1)
            folded = folded + pltpu.roll(folded, SLOT, 1)
            turned = folded.T
            below = turned[SLOT : 2 * SLOT]
            above = jnp.dot(
                turned[3 * SLOT : 4 * SLOT], flip_ref[...],
                precision=lax.Precision.HIGHEST, preferred_element_type=jnp.float32,
            )
            for first_point, value in ((LANES * b, below), (NY - LANES * (b + 1), above)):
                peer, at = divmod(first_point, out_ref.shape[-1])
                out_ref[peer, pl.ds(SLOT * i, SLOT), pl.ds(at, LANES)] = value


def criterion(field, high, low, weights, wave, peers):
    width = field.shape[-1]
    modes = width // LANES
    flip = jnp.fliplr(jnp.eye(LANES, dtype=jnp.float32))
    return pl.pallas_call(
        criterion_kernel,
        out_shape=jax.ShapeDtypeStruct((peers, SLOT * modes, NY // peers), jnp.float32),
        scratch_shapes=[pltpu.VMEM((HALF + 16, LANES), jnp.float32)] * 2,
        compiler_params=pltpu.CompilerParams(vmem_limit_bytes=LIMIT),
        name="criterion",
    )(field.reshape(NY, width), high, low, weights, wave, flip)


def local(velocity, vorticity):
    spans = lax.axis_size("gz")
    walls = lax.axis_size("gy")
    columns = NZ // (spans * walls)
    received = []
    for modes in GROUPS:
        sent = pack(velocity, vorticity, modes, spans)
        received.append(lax.all_to_all(sent, "gz", split_axis=0, concat_axis=0, tiled=True))
    high, low = tables()
    weights = degree_weights()
    index = (
        lax.axis_index("gy") * (NZ // walls)
        + lax.axis_index("gz") * columns
        + jnp.arange(LANES, dtype=jnp.int32) % SLOT
    )
    wave_z = spanwise(index)
    wave_x = (jnp.arange(KX, dtype=jnp.int32) + 1).astype(jnp.float32) / KX
    wave = wave_x[:, None] * wave_x[:, None] + wave_z[None, :] * wave_z[None, :]
    wave = jnp.broadcast_to(wave[:, None, :], (KX, 8, LANES))
    results = []
    for modes, field in zip(GROUPS, received):
        part = criterion(field, high, low, weights, wave[modes[0] : modes[-1] + 1], walls)
        part = lax.all_to_all(part, "gy", split_axis=0, concat_axis=0, tiled=True)
        part = part.reshape(walls, len(modes), SLOT, NY // walls)[:, :, :columns]
        results.append(jnp.moveaxis(part, 1, 0))
    return jnp.concatenate(results, axis=0)


def solution(mesh):
    placed = P(None, None, "gz", "gy")
    return jax.shard_map(
        local, mesh=mesh, in_specs=(placed, placed), out_specs=placed, check_vma=False
    )
```

time: 268 us -> 99.9 us (0.37); the launches traced: 263 us -> 99 us
  other arithmetic: 119 us -> 7.04 us
  local copies, waits for them, and re-layouts: 59.6 us -> 10.1 us
  matrix products: 34.8 us -> 0 us
  Pallas kernels: 0 us -> 24.4 us
  waiting for transfers between devices: 5.77 us -> 23.6 us
  blocking collectives: 11.2 us -> 0 us
    dot_general x3 -> x0, other arithmetic: 113 us -> none  [the longest x1 37.6 us: local(): jnp.einsum('cknz,jn->ckzj', field_v, slopes, precision=lax.Precision.HIGH...]
    dot_general x3 -> x0, matrix products: 34.8 us -> none  [the longest x1 12.6 us: local(): jnp.einsum('cknz,jn->ckzj', field_v, values, precision=lax.Precision.HIGH...]
    unnamed x14 -> x16, local copies, waits for them, and re-layouts: 39.5 us -> 8.43 us
    pallas_call x0 -> x5, Pallas kernels: none -> 24.4 us  [the longest x1 12 us: tables(): pl.pallas_call(table_kernel, grid=(2, HALF // rows), in_specs=[pl.BlockSp...]
    all_to_all x5 -> x0, local copies, waits for them, and re-layouts: 18.3 us -> none  [the longest x3 9.38 us: local(): lax.all_to_all(vorticity, 'gz', split_axis=3, concat_axis=2, tiled=True)]
    all_to_all x3 -> x4, waiting for transfers between devices: 5.77 us -> 23.6 us  [the longest x2 14.6 us: local(): lax.all_to_all(sent, 'gz', split_axis=0, concat_axis=0, tiled=True)]
    all_to_all x1 -> x0, blocking collectives: 11.2 us -> none  [exchange_in_pieces(): lax.all_to_all(piece, axis, split_axis=0, concat_axis=0, tiled=True)]
    all_to_all x2 -> x0, other arithmetic: 4.87 us -> none  [the longest x1 2.43 us: local(): lax.all_to_all(vorticity, 'gz', split_axis=3, concat_axis=2, tiled=True)]
  transfers between devices with their start and end apart: 3 -> 4, of which waited for: 1 -> 3; matrix products, arithmetic and copies ran while one was open for 53% -> 8% of each run, Pallas kernels for 0% -> 23%
where the time goes in v1:
time: 99.9 us; the launch traced here: 99 us
  starting transfers between devices  33.7 us (34%)
  Pallas kernels  24.4 us (24%)
  waiting for transfers between devices  23.6 us (24%)
  local copies, waits for them, and re-layouts  10.1 us (10%)
  other arithmetic  7.04 us (7%)
    all_to_all x2, starting transfers between devices, local(): lax.all_to_all(sent, 'gz', split_axis=0, concat_axis=0, tiled=True)  24.9 us
    all_to_all x2, waiting for transfers between devices, local(): lax.all_to_all(sent, 'gz', split_axis=0, concat_axis=0, tiled=True)  14.6 us
    pallas_call x1, Pallas kernels, tables(): pl.pallas_call(table_kernel, grid=(2, HALF // rows), in_specs=[pl.BlockSp...  12 us
    all_to_all x2, waiting for transfers between devices, local(): part = lax.all_to_all(part, 'gy', split_axis=0, concat_axis=0, tiled=True)  8.99 us
    pallas_call x2, Pallas kernels, criterion(): pl.pallas_call(criterion_kernel, out_shape=jax.ShapeDtypeStruct((peers, S...  8.86 us
    all_to_all x2, starting transfers between devices, local(): part = lax.all_to_all(part, 'gy', split_axis=0, concat_axis=0, tiled=True)  8.83 us
    unnamed x16, local copies, waits for them, and re-layouts  8.43 us
    pallas_call x2, Pallas kernels, pack(): pl.pallas_call(lambda *refs: pack_kernel(span // peers, *refs), grid=(1,)...  3.51 us
  transfers between devices with their start and end apart: 4, of which 3 were waited for; matrix products, arithmetic and copies ran while one was open for 8% of the time, Pallas kernels for 23%

profile of v1, /device:TPU:6, one launch (start us, length us, event | category | flops | bytes accessed | tf_op | source)
XLA Modules:
  0.0 99.0 jit_solution(817901056200440470)
XLA Ops:
  0.0 1.1 %copy-done.4 = f32[2,2,24,1920]{3,2,1,0:T(8,128)S(1)} copy-done((f32[2,2,24,1920]{3,2,1,0:T(8,128)S(1)}, f32[2,2,24,1920]{3,2,1,0:T(8,128)}, u32[]{:S(2)}) %copy-start.4) | copy-done | bytes 737304
  1.1 1.1 %copy-done.6 = f32[2,2,24,1920]{3,2,1,0:T(8,128)S(1)} copy-done((f32[2,2,24,1920]{3,2,1,0:T(8,128)S(1)}, f32[2,2,24,1920]{3,2,1,0:T(8,128)}, u32[]{:S(2)}) %copy-start.6) | copy-done | bytes 737304
  2.2 1.7 %pack.2 = f32[64,24,128]{2,1,0:T(8,128)} custom-call(f32[2,2,24,1920]{3,2,1,0:T(8,128)S(1)} %copy-done.4, f32[2,2,24,1920]{3,2,1,0:T(8,128)S(1)} %copy-done.6), custom_call_target="tpu_custom_call" | custom-call | tf_op jit(solution)/shard_map/pack/pallas_call | solution.py:52
  4.0 14.8 %all-to-all-start = ((f32[64,24,128]{2,1,0:T(8,128)}), f32[64,24,128]{2,1,0:T(8,128)S(1)}, u32[]{:S(2)}, u32[]{:S(2)}) async-start(f32[64,24,128]{2,1,0:T(8,128)} %pack.2), calls=%async_computation | async-start | bytes 1572864 | tf_op jit(solution)/shard_map/all_to_all | solution.py:173
  18.8 0.0 copy-done.5
  18.8 0.0 copy-done.7
  18.8 1.8 %pack.3 = f32[64,24,128]{2,1,0:T(8,128)} custom-call(f32[2,2,24,1920]{3,2,1,0:T(8,128)S(1)} %copy-done.5, f32[2,2,24,1920]{3,2,1,0:T(8,128)S(1)} %copy-done.7), custom_call_target="tpu_custom_call" | custom-call | tf_op jit(solution)/shard_map/pack/pallas_call | solution.py:52
  20.6 0.5 fusion.4
  21.1 2.8 %fusion.1 = (f32[2,1,768,128]{3,2,1,0:T(8,128)S(1)}, f32[2,1,768,128]{3,2,1,0:T(8,128)S(1)}) fusion(f32[1,1,768,128]{3,2,1,0:T(8,128)S(1)} %get-tuple-element.14, f32[1,1,768,128]{3,2,1,0:T(8,128)S(1)} %get-tuple-element.13), kind=kLoop, calls=%fused_computation.3 | loop fusion | flops 196608 | bytes 2359296 | tf_op jit(solution)/shard_map/cos | solution.py:83
  23.9 14.6 %all-to-all-done = f32[64,24,128]{2,1,0:T(8,128)S(1)} async-done(((f32[64,24,128]{2,1,0:T(8,128)}), f32[64,24,128]{2,1,0:T(8,128)S(1)}, u32[]{:S(2)}, u32[]{:S(2)}) %all-to-all-start) | async-done | bytes 786464 | tf_op jit(solution)/shard_map/all_to_all | solution.py:173
  38.6 10.1 %all-to-all-start.2 = ((f32[64,24,128]{2,1,0:T(8,128)}), f32[64,24,128]{2,1,0:T(8,128)S(1)}, u32[]{:S(2)}, u32[]{:S(2)}) async-start(f32[64,24,128]{2,1,0:T(8,128)} %pack.3), calls=%async_computation.2 | async-start | bytes 1572864 | tf_op jit(solution)/shard_map/all_to_all | solution.py:173
  48.6 1.5 %fusion.9 = (f32[768,128]{1,0:T(8,128)S(1)}, f32[768,128]{1,0:T(8,128)S(1)}) fusion(s32[768]{0:T(1024)S(1)} %get-tuple-element.17, s32[768]{0:T(1024)S(1)} %get-tuple-element.18, pred[768]{0:T(1024)(128)(4,1)S(1)} %compare_and_fusion), kind=kLoop, calls=%fused_computation.15 | loop fusion | flops 294912 | bytes 793344 | tf_op jit(solution)/shard_map/cos | solution.py:83
  50.2 0.1 stack.28
  50.2 0.1 stack.29
  50.3 1.8 %pad_maximum_fusion.base_ref = f32[2,4,768,128]{3,2,1,0:T(8,128)} fusion(f32[2,1,768,128]{3,2,1,0:T(8,128)S(1)} %stack.29, f32[2,1,768,128]{3,2,1,0:T(8,128)S(1)} %stack.28, f32[2,1,768,128]{3,2,1,0:T(8,128)S(1)} %get-tuple-element.10, f32[2,1,768,128]{3,2,1,0:T(8,128)S(1)} %get-tuple-element.9), kind=kLoop, calls=%fused_computation | loop fusion | flops 2359296 | bytes 6291456 | tf_op jit(solution)/shard_map/stack | solution.py:83
  52.1 12.0 %tables.1 = (bf16[2,768,768]{2,1,0:T(8,128)(2,1)S(1)}, bf16[2,768,768]{2,1,0:T(8,128)(2,1)S(1)}) custom-call(f32[2,4,768,128]{3,2,1,0:T(8,128)} %pad_maximum_fusion.base_ref), custom_call_target="tpu_custom_call" | custom-call | tf_op jit(solution)/shard_map/tables/pallas_call | solution.py:86
  64.2 1.4 %copy-done = bf16[2,768,768]{2,1,0:T(8,128)(2,1)} copy-done((bf16[2,768,768]{2,1,0:T(8,128)(2,1)}, bf16[2,768,768]{2,1,0:T(8,128)(2,1)S(1)}, u32[]{:S(2)}) %copy-start) | copy-done | bytes 2359320
  65.6 1.4 %copy-done.3 = bf16[2,768,768]{2,1,0:T(8,128)(2,1)} copy-done((bf16[2,768,768]{2,1,0:T(8,128)(2,1)}, bf16[2,768,768]{2,1,0:T(8,128)(2,1)S(1)}, u32[]{:S(2)}) %copy-start.3) | copy-done | bytes 2359320
  67.1 0.2 sine_multiply_fusion
  67.3 0.1 rev.5.flip_ref
  67.4 0.1 broadcast_add_fusion.1
  67.5 0.5 broadcast_in_dim.6.weight_ref
  68.0 1.7 %copy-done.1 = bf16[2,768,768]{2,1,0:T(8,128)(2,1)S(1)} copy-done((bf16[2,768,768]{2,1,0:T(8,128)(2,1)S(1)}, bf16[2,768,768]{2,1,0:T(8,128)(2,1)}, u32[]{:S(2)}) %copy-start.1) | copy-done | bytes 2359320
  69.6 4.4 %criterion.2 = f32[4,32,384]{2,1,0:T(8,128)} custom-call(f32[1536,128]{1,0:T(8,128)S(1)} %bitcast.16, bf16[2,768,768]{2,1,0:T(8,128)(2,1)S(1)} %copy-done.1, bf16[2,768,768]{2,1,0:T(8,128)(2,1)} %copy-done.3, f32[2,2,768,128]{3,2,1,0:T(8,128)S(1)} %broadcast_in_dim.6.weight_ref, f32[1,8,128]{2,1,0:T(8,128)S(1)} %broadcast_in_dim.7.wave_ref, ...), custom_call_target="tpu_custom_call" | custom-call | tf_op jit(solution)/shard_map/criterion/pallas_call | solution.py:157
  74.1 0.0 all-to-all-done.2
  74.1 5.4 %all-to-all-start.1 = ((f32[4,32,384]{2,1,0:T(8,128)}), f32[4,32,384]{2,1,0:T(8,128)S(1)}, u32[]{:S(2)}, u32[]{:S(2)}) async-start(f32[4,32,384]{2,1,0:T(8,128)} %criterion.2), calls=%async_computation.1 | async-start | bytes 393216 | tf_op jit(solution)/shard_map/all_to_all | solution.py:188
  79.5 1.7 %copy-done.2 = bf16[2,768,768]{2,1,0:T(8,128)(2,1)S(1)} copy-done((bf16[2,768,768]{2,1,0:T(8,128)(2,1)S(1)}, bf16[2,768,768]{2,1,0:T(8,128)(2,1)}, u32[]{:S(2)}) %copy-start.2) | copy-done | bytes 2359320
  81.2 4.4 %criterion.3 = f32[4,32,384]{2,1,0:T(8,128)} custom-call(f32[1536,128]{1,0:T(8,128)S(1)} %bitcast.17, bf16[2,768,768]{2,1,0:T(8,128)(2,1)S(1)} %copy-done.2, bf16[2,768,768]{2,1,0:T(8,128)(2,1)} %copy-done.3, f32[2,2,768,128]{3,2,1,0:T(8,128)S(1)} %broadcast_in_dim.6.weight_ref, f32[1,8,128]{2,1,0:T(8,128)S(1)} %broadcast_in_dim.8.wave_ref, ...), custom_call_target="tpu_custom_call" | custom-call | tf_op jit(solution)/shard_map/criterion/pallas_call | solution.py:157
  85.6 1.7 %all-to-all-done.1 = f32[4,32,384]{2,1,0:T(8,128)S(1)} async-done(((f32[4,32,384]{2,1,0:T(8,128)}), f32[4,32,384]{2,1,0:T(8,128)S(1)}, u32[]{:S(2)}, u32[]{:S(2)}) %all-to-all-start.1) | async-done | bytes 196640 | tf_op jit(solution)/shard_map/all_to_all | solution.py:188
  87.3 3.4 %all-to-all-start.3 = ((f32[4,32,384]{2,1,0:T(8,128)}), f32[4,32,384]{2,1,0:T(8,128)S(1)}, u32[]{:S(2)}, u32[]{:S(2)}) async-start(f32[4,32,384]{2,1,0:T(8,128)} %criterion.3), calls=%async_computation.3 | async-start | bytes 393216 | tf_op jit(solution)/shard_map/all_to_all | solution.py:188
  90.7 7.3 %all-to-all-done.3 = f32[4,32,384]{2,1,0:T(8,128)S(1)} async-done(((f32[4,32,384]{2,1,0:T(8,128)}), f32[4,32,384]{2,1,0:T(8,128)S(1)}, u32[]{:S(2)}, u32[]{:S(2)}) %all-to-all-start.3) | async-done | bytes 196640 | tf_op jit(solution)/shard_map/all_to_all | solution.py:188
  98.1 1.0 copy.5
  (23 shorter events, 0.2 us)
Async XLA Ops:
  0.0 1.1 %copy-start.4 = (f32[2,2,24,1920]{3,2,1,0:T(8,128)S(1)}, f32[2,2,24,1920]{3,2,1,0:T(8,128)}, u32[]{:S(2)}) copy-start(f32[2,2,24,1920]{3,2,1,0:T(8,128)} %refs_0_.3) | copy-start | bytes 2211844
  1.1 1.1 %copy-start.6 = (f32[2,2,24,1920]{3,2,1,0:T(8,128)S(1)}, f32[2,2,24,1920]{3,2,1,0:T(8,128)}, u32[]{:S(2)}) copy-start(f32[2,2,24,1920]{3,2,1,0:T(8,128)} %refs_1_.3) | copy-start | bytes 2211844
  2.2 16.6 %copy-start.5 = (f32[2,2,24,1920]{3,2,1,0:T(8,128)S(1)}, f32[2,2,24,1920]{3,2,1,0:T(8,128)}, u32[]{:S(2)}) copy-start(f32[2,2,24,1920]{3,2,1,0:T(8,128)} %refs_0_.3) | copy-start | bytes 2211844
  2.2 16.6 %copy-start.7 = (f32[2,2,24,1920]{3,2,1,0:T(8,128)S(1)}, f32[2,2,24,1920]{3,2,1,0:T(8,128)}, u32[]{:S(2)}) copy-start(f32[2,2,24,1920]{3,2,1,0:T(8,128)} %refs_1_.3) | copy-start | bytes 2211844
  4.0 34.6 %all-to-all-start = ((f32[64,24,128]{2,1,0:T(8,128)}), f32[64,24,128]{2,1,0:T(8,128)S(1)}, u32[]{:S(2)}, u32[]{:S(2)}) async-start(f32[64,24,128]{2,1,0:T(8,128)} %pack.2), calls=%async_computation | async-start | bytes 1572864 | tf_op jit(solution)/shard_map/all_to_all | solution.py:173
  38.6 35.5 %all-to-all-start.2 = ((f32[64,24,128]{2,1,0:T(8,128)}), f32[64,24,128]{2,1,0:T(8,128)S(1)}, u32[]{:S(2)}, u32[]{:S(2)}) async-start(f32[64,24,128]{2,1,0:T(8,128)} %pack.3), calls=%async_computation.2 | async-start | bytes 1572864 | tf_op jit(solution)/shard_map/all_to_all | solution.py:173
  64.2 1.4 %copy-start = (bf16[2,768,768]{2,1,0:T(8,128)(2,1)}, bf16[2,768,768]{2,1,0:T(8,128)(2,1)S(1)}, u32[]{:S(2)}) copy-start(bf16[2,768,768]{2,1,0:T(8,128)(2,1)S(1)} %get-tuple-element.7.hi_ref) | copy-start | bytes 7077892
  65.6 1.4 %copy-start.3 = (bf16[2,768,768]{2,1,0:T(8,128)(2,1)}, bf16[2,768,768]{2,1,0:T(8,128)(2,1)S(1)}, u32[]{:S(2)}) copy-start(bf16[2,768,768]{2,1,0:T(8,128)(2,1)S(1)} %get-tuple-element.8.lo_ref) | copy-start | bytes 7077892
  68.0 1.7 %copy-start.1 = (bf16[2,768,768]{2,1,0:T(8,128)(2,1)S(1)}, bf16[2,768,768]{2,1,0:T(8,128)(2,1)}, u32[]{:S(2)}) copy-start(bf16[2,768,768]{2,1,0:T(8,128)(2,1)} %copy-done) | copy-start | bytes 7077892
  74.1 13.2 %all-to-all-start.1 = ((f32[4,32,384]{2,1,0:T(8,128)}), f32[4,32,384]{2,1,0:T(8,128)S(1)}, u32[]{:S(2)}, u32[]{:S(2)}) async-start(f32[4,32,384]{2,1,0:T(8,128)} %criterion.2), calls=%async_computation.1 | async-start | bytes 393216 | tf_op jit(solution)/shard_map/all_to_all | solution.py:188
  79.5 1.7 %copy-start.2 = (bf16[2,768,768]{2,1,0:T(8,128)(2,1)S(1)}, bf16[2,768,768]{2,1,0:T(8,128)(2,1)}, u32[]{:S(2)}) copy-start(bf16[2,768,768]{2,1,0:T(8,128)(2,1)} %copy-done) | copy-start | bytes 7077892
  87.3 10.7 %all-to-all-start.3 = ((f32[4,32,384]{2,1,0:T(8,128)}), f32[4,32,384]{2,1,0:T(8,128)S(1)}, u32[]{:S(2)}, u32[]{:S(2)}) async-start(f32[4,32,384]{2,1,0:T(8,128)} %criterion.3), calls=%async_computation.3 | async-start | bytes 393216 | tf_op jit(solution)/shard_map/all_to_all | solution.py:188

commit v2 on v0

v2 whole, which is shorter than its diff:
```python
import math

import jax
import jax.numpy as jnp
from jax import lax
from jax.experimental import pallas as pl
from jax.experimental.pallas import tpu as pltpu
from jax.sharding import Mesh
from jax.sharding import PartitionSpec as P

NY = 1536
NZ = 7680
KX = 2
HALF = NY // 2
SLOT = 32
LANES = 128
LIMIT = 24 * 1024 * 1024
SPANS = ("x", "y", "half", "core")
ROUTE = ("half", "y", "x", "core")
SIZES = {"x": 4, "y": 4, "half": 2, "core": 2}


def routes():
    places = []
    for a in range(math.prod(SIZES.values())):
        rest, at = a, {}
        for name in reversed(SPANS):
            rest, at[name] = divmod(rest, SIZES[name])
        place = 0
        for name in ROUTE:
            place = place * SIZES[name] + at[name]
        places.append(place)
    return places


def spanwise(index):
    signed = jnp.where(index < NZ // 2, index, index - NZ)
    return signed.astype(jnp.float32) * (2.0 / NZ)


def pack_kernel(places, cols, v_hbm, o_hbm, out_ref, v_buf, o_buf, sems):
    _, modes, rows, span = v_buf.shape
    chunks = span // LANES
    copies = []
    for t in range(rows // 8):
        at = pl.ds(8 * t, 8)
        pair = [
            pltpu.make_async_copy(src.at[:, :, at, :], dst.at[:, :, at, :], sems.at[t, f])
            for f, (src, dst) in enumerate(((v_hbm, v_buf), (o_hbm, o_buf)))
        ]
        for copy in pair:
            copy.start()
        copies.append(pair)
    lane = lax.broadcasted_iota(jnp.int32, (8, LANES), 1)
    for t in range(rows // 8):
        at = pl.ds(8 * t, 8)
        for copy in copies[t]:
            copy.wait()
        turned = {}

        def tile(m, g, k):
            if (m, g, k) not in turned:
                ref = (v_buf, o_buf)[g // 2]
                value = ref[g % 2, m, at, pl.ds(LANES * (k % chunks), LANES)]
                turned[m, g, k] = pltpu.roll(value, SLOT * g, 1) if g else value
            return turned[m, g, k]

        for a, place in enumerate(places):
            k, off = divmod(cols * a, LANES)
            own = (lane - off) & (LANES - 1)
            for m in range(modes):
                merged = [tile(m, 0, k + s) for s in range(2 if off + cols > LANES else 1)]
                for g in range(1, 4):
                    merged = [jnp.where(own >= SLOT * g, tile(m, g, k + s), v) for s, v in enumerate(merged)]
                value = merged[0]
                if len(merged) > 1:
                    value = jnp.where((own & (SLOT - 1)) < LANES - off, value, merged[1])
                out_ref[place, pl.ds(8 * t * modes + m, 8, stride=modes), :] = value


def pack(velocity, vorticity, places):
    _, modes, rows, span = velocity.shape
    peers = len(places)
    return pl.pallas_call(
        lambda *refs: pack_kernel(places, span // peers, *refs),
        in_specs=[pl.BlockSpec(memory_space=pltpu.HBM)] * 2,
        out_shape=jax.ShapeDtypeStruct((peers, rows * modes, LANES), jnp.float32),
        scratch_shapes=[pltpu.VMEM(velocity.shape, jnp.float32)] * 2
        + [pltpu.SemaphoreType.DMA((rows // 8, 2))],
        compiler_params=pltpu.CompilerParams(vmem_limit_bytes=LIMIT),
        name="pack",
    )(*(pltpu.with_memory_space_constraint(x, pltpu.HBM) for x in (velocity, vorticity)))


def table_kernel(base_ref, hi_ref, lo_ref):
    rows = 32

    def block(i, carry):
        at = pl.ds(pl.multiple_of(i * rows, rows), rows)
        for parity in range(2):
            c, s, turn_c, turn_s = (base_ref[parity, k, at, :] for k in range(4))
            for q in range(HALF // LANES):
                lanes = pl.ds(LANES * q, LANES)
                hi_ref[parity, at, lanes], lo_ref[parity, at, lanes] = halves_of(c)
                c, s = c * turn_c - s * turn_s, s * turn_c + c * turn_s
        return carry

    lax.fori_loop(0, HALF // rows, block, 0)


def tables():
    point = jnp.arange(HALF, dtype=jnp.int32)[:, None]
    first = 2 * jnp.arange(LANES, dtype=jnp.int32)[None, :]
    turn = jnp.full((1, LANES), 2 * LANES, jnp.int32)

    def angle(degree):
        return (degree * (2 * point + 1) % (4 * NY)).astype(jnp.float32) * (math.pi / (2 * NY))

    degrees = jnp.stack([angle(first), angle(first + 1)])
    turns = jnp.broadcast_to(angle(turn), degrees.shape)
    base = jnp.stack([jnp.cos(degrees), jnp.sin(degrees), jnp.cos(turns), jnp.sin(turns)], axis=1)
    return pl.pallas_call(
        table_kernel,
        out_shape=[jax.ShapeDtypeStruct((2, HALF, HALF), jnp.bfloat16)] * 2,
        compiler_params=pltpu.CompilerParams(vmem_limit_bytes=LIMIT),
        name="tables",
    )(base)


def factors(own, first):
    normal = own < 2 * SLOT
    wave_z = spanwise(first + own % SLOT)
    wave_x = (jnp.arange(KX, dtype=jnp.int32) + 1).astype(jnp.float32) / KX
    wave = wave_x[:, None] * wave_x[:, None] + wave_z[None, :] * wave_z[None, :]
    degree = jnp.arange(NY, dtype=jnp.int32).reshape(HALF, 2).T.astype(jnp.float32)
    scaled = degree * (math.pi / NY)
    stretch = (scaled * jnp.sin(scaled))[:, :, None]
    edge = (-0.5 * scaled * jnp.sin(0.5 * scaled))[:, :, None]
    by_degree = jnp.where(normal, jnp.stack([stretch, edge]), 0.0)
    shift = jnp.where(normal, wave, 1.0)
    square = jnp.where(normal, 0.25 / wave, 0.25)
    slope = jnp.where(normal, 0.0, 0.0625 / wave)
    rows = jnp.broadcast_to(jnp.stack([shift, square, slope], axis=1)[:, :, None, :], (KX, 3, 8, LANES))
    lane = jnp.arange(LANES, dtype=jnp.int32)
    part = jnp.arange(4, dtype=jnp.int32)
    pick = (own[None, :, None] % SLOT == lane % SLOT) & (lane // SLOT == part[:, None, None])
    flip = lane[:, None] + lane[None, :] == LANES - 1
    return by_degree, rows, pick.astype(jnp.bfloat16), flip.astype(jnp.bfloat16)


def halves_of(value):
    high = value.astype(jnp.bfloat16)
    return high, (value - high.astype(jnp.float32)).astype(jnp.bfloat16)


def product(a, b):
    return jnp.dot(a, b, preferred_element_type=jnp.float32)


def criterion_kernel(
    places, x_ref, hi_hbm, lo_hbm, degree_ref, rows_ref, pick_ref, flip_ref, out_ref,
    hi_ref, lo_ref, xh_ref, xl_ref, low_ref, top_ref, sems,
):
    copies = [
        pltpu.make_async_copy(src.at[parity], dst.at[parity], sems.at[parity, k])
        for parity in range(2)
        for k, (src, dst) in enumerate(((hi_hbm, hi_ref), (lo_hbm, lo_ref)))
    ]
    for copy in copies:
        copy.start()
    modes = x_ref.shape[0] // NY
    pair = 2 * NY // len(places)
    sums = []
    for parity in range(2):
        for m in range(modes):
            lanes = pl.ds(LANES * m, LANES)
            total = jnp.zeros((pair // 2, LANES), jnp.float32)
            shift = rows_ref[m, 0, :1]
            for c in range(NY // pair):
                at = pl.ds(c * pair // 2, pair // 2)
                first = places[2 * c] * (pair // 2) * modes + parity * modes + m
                x = x_ref[pl.ds(first, pair // 2, stride=2 * modes), :]
                total = total + x * degree_ref[1, parity, at, :]
                high, low = halves_of(x * (shift + degree_ref[0, parity, at, :]))
                xh_ref[parity, at, lanes] = high
                xl_ref[parity, at, lanes] = low
            sums.append(jnp.sum(total, axis=0, keepdims=True))
    for copy in copies:
        copy.wait()
    halves = []
    for parity in range(2):
        xh = xh_ref[parity]
        halves.append(
            product(hi_ref[parity], xh) + product(hi_ref[parity], xl_ref[parity]) + product(lo_ref[parity], xh)
        )
    low_ref[pl.ds(8, HALF), :] = halves[0] + halves[1]
    top_ref[pl.ds(8, HALF), :] = halves[0] - halves[1]
    for m in range(modes):
        lanes = pl.ds(LANES * m, LANES)
        even, odd = sums[m], sums[modes + m]
        low_ref[pl.ds(8, 1), lanes] = low_ref[pl.ds(8, 1), lanes] + (even + odd)
        top_ref[pl.ds(8, 1), lanes] = top_ref[pl.ds(8, 1), lanes] + (even - odd)
    outside = jnp.zeros((8, LANES * modes), jnp.float32)
    low_ref[pl.ds(0, 8), :] = outside
    top_ref[pl.ds(0, 8), :] = outside
    low_ref[pl.ds(8 + HALF, 1), :] = top_ref[pl.ds(7 + HALF, 1), :]
    top_ref[pl.ds(8 + HALF, 1), :] = low_ref[pl.ds(7 + HALF, 1), :]
    above = []
    for b in range(HALF // LANES):
        result = None
        for part in range(2 * modes):
            ref, m = (low_ref, top_ref)[part // modes], part % modes
            lanes = pl.ds(LANES * m, LANES)
            here = ref[pl.ds(8 + LANES * b, LANES), lanes]
            slope = ref[pl.ds(9 + LANES * b, LANES), lanes] - ref[pl.ds(7 + LANES * b, LANES), lanes]
            value = here * here * rows_ref[m, 1, :1] + slope * slope * rows_ref[m, 2, :1]
            high, low = halves_of(value)
            added = product(high, pick_ref[part]) + product(low, pick_ref[part])
            result = added if result is None else result + added
        turned = result.T
        peer, at = divmod(LANES * b, out_ref.shape[-1])
        out_ref[peer, :, pl.ds(at, LANES)] = turned[: SLOT * modes]
        high, low = halves_of(turned[SLOT * modes :])
        peer, at = divmod(NY - LANES * (b + 1), out_ref.shape[-1])
        out_ref[peer, :, pl.ds(at, LANES)] = product(high, flip_ref[...]) + product(low, flip_ref[...])


def criterion(field, high, low, numbers, places, peers):
    modes = field.shape[1] * len(places) // NY
    width = LANES * modes
    fast, slow = pl.BlockSpec(memory_space=pltpu.VMEM), pl.BlockSpec(memory_space=pltpu.HBM)
    call = pl.pallas_call(
        lambda *refs: criterion_kernel(places, *refs),
        in_specs=[fast, slow, slow, fast, fast, fast, fast],
        out_shape=jax.ShapeDtypeStruct((peers, SLOT * modes, NY // peers), jnp.float32),
        scratch_shapes=[pltpu.VMEM(high.shape, jnp.bfloat16)] * 2
        + [pltpu.VMEM((2, HALF, width), jnp.bfloat16)] * 2
        + [pltpu.VMEM((HALF + 16, width), jnp.float32)] * 2
        + [pltpu.SemaphoreType.DMA((2, 2))],
        compiler_params=pltpu.CompilerParams(vmem_limit_bytes=LIMIT),
        name="criterion",
    )
    high, low = (pltpu.with_memory_space_constraint(x, pltpu.HBM) for x in (high, low))
    return call(field.reshape(NY * modes, LANES), high, low, *numbers)


def local(velocity, vorticity):
    walls = lax.axis_size("gy")
    places = routes()
    columns = NZ // (len(places) * walls)
    sent = pack(velocity, vorticity, places)
    field = lax.all_to_all(sent, ROUTE, split_axis=0, concat_axis=0, tiled=True)
    high, low = tables()
    start = lax.axis_index(SPANS) * columns
    own = (jnp.arange(LANES, dtype=jnp.int32) - start) % LANES
    numbers = factors(own, lax.axis_index("gy") * (NZ // walls) + start)
    part = criterion(field, high, low, numbers, places, walls)
    part = lax.all_to_all(part, "gy", split_axis=0, concat_axis=0, tiled=True)
    part = part.reshape(walls, KX, SLOT, NY // walls)[:, :, :columns]
    return jnp.moveaxis(part, 1, 0)


def solution(mesh):
    fine = Mesh(mesh.devices.reshape(*SIZES.values(), -1), (*SIZES, "gy"))
    placed = P(None, None, SPANS, "gy")
    return jax.shard_map(
        local, mesh=fine, in_specs=(placed, placed), out_specs=placed, check_vma=False
    )
```

time: 268 us -> 82.4 us (0.31); the launches traced: 263 us -> 81.7 us
  other arithmetic: 119 us -> 6.04 us
  local copies, waits for them, and re-layouts: 59.6 us -> 3.9 us
  matrix products: 34.8 us -> 0 us
  waiting for transfers between devices: 5.77 us -> 28.5 us
  starting transfers between devices: 31.8 us -> 14.6 us
  Pallas kernels: 0 us -> 11 us
  blocking collectives: 11.2 us -> 17.4 us
    dot_general x3 -> x0, other arithmetic: 113 us -> none  [the longest x1 37.6 us: local(): jnp.einsum('cknz,jn->ckzj', field_v, slopes, precision=lax.Precision.HIGH...]
    unnamed x14 -> x5, local copies, waits for them, and re-layouts: 39.5 us -> 3.79 us
    dot_general x3 -> x0, matrix products: 34.8 us -> none  [the longest x1 12.6 us: local(): jnp.einsum('cknz,jn->ckzj', field_v, values, precision=lax.Precision.HIGH...]
    all_to_all x3 -> x1, waiting for transfers between devices: 5.77 us -> 28.5 us  [local(): field = lax.all_to_all(sent, ROUTE, split_axis=0, concat_axis=0, tiled=True)]
    all_to_all x5 -> x0, local copies, waits for them, and re-layouts: 18.3 us -> none  [the longest x3 9.38 us: local(): lax.all_to_all(vorticity, 'gz', split_axis=3, concat_axis=2, tiled=True)]
    all_to_all x3 -> x1, starting transfers between devices: 31.8 us -> 14.6 us  [local(): field = lax.all_to_all(sent, ROUTE, split_axis=0, concat_axis=0, tiled=True)]
    pallas_call x0 -> x3, Pallas kernels: none -> 11 us  [the longest x1 6.52 us: criterion(): return call(field.reshape(NY * modes, LANES), high, low, *numbers)]
    all_to_all x1, blocking collectives: 11.2 us -> 17.4 us  [local(): part = lax.all_to_all(part, 'gy', split_axis=0, concat_axis=0, tiled=True)]
  transfers between devices with their start and end apart: 3 -> 1, of which waited for: 1 -> 1; matrix products, arithmetic and copies ran while one was open for 53% -> 8% of each run, Pallas kernels for 0% -> 2%
where the time goes in v2:
time: 82.4 us; the launch traced here: 81.7 us
  waiting for transfers between devices  28.5 us (35%)
  blocking collectives  17.4 us (21%)
  starting transfers between devices  14.6 us (18%)
  Pallas kernels  11 us (13%)
  other arithmetic  6.04 us (7%)
  local copies, waits for them, and re-layouts  3.9 us (5%)
    all_to_all x1, waiting for transfers between devices, local(): field = lax.all_to_all(sent, ROUTE, split_axis=0, concat_axis=0, tiled=True)  28.5 us
    all_to_all x1, blocking collectives, local(): part = lax.all_to_all(part, 'gy', split_axis=0, concat_axis=0, tiled=True)  17.4 us
    all_to_all x1, starting transfers between devices, local(): field = lax.all_to_all(sent, ROUTE, split_axis=0, concat_axis=0, tiled=True)  14.6 us
    pallas_call x1, Pallas kernels, criterion(): return call(field.reshape(NY * modes, LANES), high, low, *numbers)  6.52 us
    unnamed x5, local copies, waits for them, and re-layouts  3.79 us
    pallas_call x1, Pallas kernels, pack(): pl.pallas_call(lambda *refs: pack_kernel(places, span // peers, *refs), i...  2.93 us
    cos x1, other arithmetic, tables(): jnp.cos(degrees)  2.78 us
  transfers between devices with their start and end apart: 1, of which 1 were waited for; matrix products, arithmetic and copies ran while one was open for 8% of the time, Pallas kernels for 2%

profile of v2, /device:TPU:6, one launch (start us, length us, event | category | flops | bytes accessed | tf_op | source)
XLA Modules:
  0.0 81.7 jit_solution(6722383077198744978)
XLA Ops:
  0.0 2.9 %pack.1 = f32[64,48,128]{2,1,0:T(8,128)} custom-call(f32[2,2,24,1920]{3,2,1,0:T(8,128)} %refs_0_.1, f32[2,2,24,1920]{3,2,1,0:T(8,128)} %refs_1_.1), custom_call_target="tpu_custom_call" | custom-call | tf_op jit(solution)/shard_map/pack/pallas_call | solution.py:84
  2.9 14.6 %all-to-all-start = ((f32[64,48,128]{2,1,0:T(8,128)}), f32[64,48,128]{2,1,0:T(8,128)S(1)}, u32[]{:S(2)}, u32[]{:S(2)}) async-start(f32[64,48,128]{2,1,0:T(8,128)} %pack.1), calls=%async_computation | async-start | bytes 3145728 | tf_op jit(solution)/shard_map/all_to_all | solution.py:252
  17.6 0.5 fusion.4
  18.1 2.8 %fusion.1 = (f32[2,1,768,128]{3,2,1,0:T(8,128)S(1)}, f32[2,1,768,128]{3,2,1,0:T(8,128)S(1)}) fusion(f32[1,1,768,128]{3,2,1,0:T(8,128)S(1)} %get-tuple-element.14, f32[1,1,768,128]{3,2,1,0:T(8,128)S(1)} %get-tuple-element.13), kind=kLoop, calls=%fused_computation.4 | loop fusion | flops 196608 | bytes 2359296 | tf_op jit(solution)/shard_map/cos | solution.py:121
  20.9 1.5 %fusion.9 = (f32[768,128]{1,0:T(8,128)S(1)}, f32[768,128]{1,0:T(8,128)S(1)}) fusion(s32[768]{0:T(1024)S(1)} %get-tuple-element.18, s32[768]{0:T(1024)S(1)} %get-tuple-element.19, pred[768]{0:T(1024)(128)(4,1)S(1)} %compare_and_fusion), kind=kLoop, calls=%fused_computation.15 | loop fusion | flops 294912 | bytes 793344 | tf_op jit(solution)/shard_map/cos | solution.py:121
  22.5 0.1 stack.33
  22.5 0.1 stack.32
  22.6 0.2 pad_maximum_fusion.base_ref
  22.8 1.6 %tables.1 = (bf16[2,768,768]{2,1,0:T(8,128)(2,1)S(1)}, bf16[2,768,768]{2,1,0:T(8,128)(2,1)S(1)}) custom-call(f32[2,4,768,128]{3,2,1,0:T(8,128)S(1)} %pad_maximum_fusion.base_ref), custom_call_target="tpu_custom_call" | custom-call | tf_op jit(solution)/shard_map/tables/pallas_call | solution.py:122
  24.4 0.0 copy-start
  24.4 1.4 %copy-done = bf16[2,768,768]{2,1,0:T(8,128)(2,1)} copy-done((bf16[2,768,768]{2,1,0:T(8,128)(2,1)}, bf16[2,768,768]{2,1,0:T(8,128)(2,1)S(1)}, u32[]{:S(2)}) %copy-start) | copy-done | bytes 2359320
  25.8 0.0 copy-start.1
  25.8 1.4 %copy-done.1 = bf16[2,768,768]{2,1,0:T(8,128)(2,1)} copy-done((bf16[2,768,768]{2,1,0:T(8,128)(2,1)}, bf16[2,768,768]{2,1,0:T(8,128)(2,1)S(1)}, u32[]{:S(2)}) %copy-start.1) | copy-done | bytes 2359320
  27.3 0.1 broadcast_select_fusion.3
  27.4 0.2 sine_multiply_fusion
  27.6 0.1 broadcast_compare_fusion
  27.8 0.5 broadcast_select_fusion.refs_3_
  28.2 28.5 %all-to-all-done = f32[64,48,128]{2,1,0:T(8,128)S(1)} async-done(((f32[64,48,128]{2,1,0:T(8,128)}), f32[64,48,128]{2,1,0:T(8,128)S(1)}, u32[]{:S(2)}, u32[]{:S(2)}) %all-to-all-start) | async-done | bytes 1572896 | tf_op jit(solution)/shard_map/all_to_all | solution.py:252
  56.8 6.5 %criterion.1 = f32[4,64,384]{2,1,0:T(8,128)S(1)} custom-call(f32[3072,128]{1,0:T(8,128)S(1)} %bitcast.12, bf16[2,768,768]{2,1,0:T(8,128)(2,1)} %copy-done, bf16[2,768,768]{2,1,0:T(8,128)(2,1)} %copy-done.1, f32[2,2,768,128]{3,2,1,0:T(8,128)S(1)} %broadcast_select_fusion.refs_3_, f32[2,3,8,128]{3,2,1,0:T(8,128)S(1)} %broadcast_in_dim.60.refs_4_, ...), custom_call_target="tpu_custom_call" | custom-call | tf_op jit(solution)/shard_map/criterion/pallas_call | solution.py:244
  63.3 17.4 %all_to_all.10 = f32[4,64,384]{2,1,0:T(8,128)S(1)} all-to-all(f32[4,64,384]{2,1,0:T(8,128)S(1)} %criterion.1), channel_id=1, replica_groups=mesh['x'=4,'y'=4,'half'=2,'core'=2,'gy'=4] {'gy'}, dimensions={0} | all-to-all | bytes 786432 | tf_op jit(solution)/shard_map/all_to_all | solution.py:258
  80.7 1.0 %copy.6 = f32[4,2,30,384]{3,0,2,1:T(4,128)} copy(f32[4,2,30,384]{3,2,1,0:T(8,128)S(1)} %bitcast.13) | data formatting | bytes 737280
  (15 shorter events, 0.2 us)
Async XLA Ops:
  2.9 53.8 %all-to-all-start = ((f32[64,48,128]{2,1,0:T(8,128)}), f32[64,48,128]{2,1,0:T(8,128)S(1)}, u32[]{:S(2)}, u32[]{:S(2)}) async-start(f32[64,48,128]{2,1,0:T(8,128)} %pack.1), calls=%async_computation | async-start | bytes 3145728 | tf_op jit(solution)/shard_map/all_to_all | solution.py:252
  24.4 1.4 %copy-start = (bf16[2,768,768]{2,1,0:T(8,128)(2,1)}, bf16[2,768,768]{2,1,0:T(8,128)(2,1)S(1)}, u32[]{:S(2)}) copy-start(bf16[2,768,768]{2,1,0:T(8,128)(2,1)S(1)} %get-tuple-element.7.refs_1_) | copy-start | bytes 7077892
  25.8 1.4 %copy-start.1 = (bf16[2,768,768]{2,1,0:T(8,128)(2,1)}, bf16[2,768,768]{2,1,0:T(8,128)(2,1)S(1)}, u32[]{:S(2)}) copy-start(bf16[2,768,768]{2,1,0:T(8,128)(2,1)S(1)} %get-tuple-element.8.refs_2_) | copy-start | bytes 7077892

commit v3 on v2

--- a/solution.py
+++ b/solution.py
@@ -14,6 +14,7 @@
 HALF = NY // 2
 SLOT = 32
 LANES = 128
+BLOCK = 384
 LIMIT = 24 * 1024 * 1024
 SPANS = ("x", "y", "half", "core")
 ROUTE = ("half", "y", "x", "core")
@@ -38,7 +39,7 @@
     return signed.astype(jnp.float32) * (2.0 / NZ)
 
 
-def pack_kernel(places, cols, v_hbm, o_hbm, out_ref, v_buf, o_buf, sems):
+def pack_kernel(places, cols, v_hbm, o_hbm, out_hbm, v_buf, o_buf, out_ref, sems):
     _, modes, rows, span = v_buf.shape
     chunks = span // LANES
     copies = []
@@ -52,6 +53,7 @@
             copy.start()
         copies.append(pair)
     lane = lax.broadcasted_iota(jnp.int32, (8, LANES), 1)
+    leaving = []
     for t in range(rows // 8):
         at = pl.ds(8 * t, 8)
         for copy in copies[t]:
@@ -76,6 +78,11 @@
                 if len(merged) > 1:
                     value = jnp.where((own & (SLOT - 1)) < LANES - off, value, merged[1])
                 out_ref[place, pl.ds(8 * t * modes + m, 8, stride=modes), :] = value
+        done = pl.ds(8 * t * modes, 8 * modes)
+        leaving.append(pltpu.make_async_copy(out_ref.at[:, done, :], out_hbm.at[:, done, :], sems.at[t, 2]))
+        leaving[-1].start()
+    for copy in leaving:
+        copy.wait()
 
 
 def pack(velocity, vorticity, places):
@@ -84,9 +91,10 @@
     return pl.pallas_call(
         lambda *refs: pack_kernel(places, span // peers, *refs),
         in_specs=[pl.BlockSpec(memory_space=pltpu.HBM)] * 2,
+        out_specs=pl.BlockSpec(memory_space=pltpu.HBM),
         out_shape=jax.ShapeDtypeStruct((peers, rows * modes, LANES), jnp.float32),
         scratch_shapes=[pltpu.VMEM(velocity.shape, jnp.float32)] * 2
-        + [pltpu.SemaphoreType.DMA((rows // 8, 2))],
+        + [pltpu.VMEM((peers, rows * modes, LANES), jnp.float32), pltpu.SemaphoreType.DMA((rows // 8, 3))],
         compiler_params=pltpu.CompilerParams(vmem_limit_bytes=LIMIT),
         name="pack",
     )(*(pltpu.with_memory_space_constraint(x, pltpu.HBM) for x in (velocity, vorticity)))
@@ -138,12 +146,13 @@
     edge = (-0.5 * scaled * jnp.sin(0.5 * scaled))[:, :, None]
     by_degree = jnp.where(normal, jnp.stack([stretch, edge]), 0.0)
     shift = jnp.where(normal, wave, 1.0)
-    square = jnp.where(normal, 0.25 / wave, 0.25)
-    slope = jnp.where(normal, 0.0, 0.0625 / wave)
-    rows = jnp.broadcast_to(jnp.stack([shift, square, slope], axis=1)[:, :, None, :], (KX, 3, 8, LANES))
+    size = jnp.where(normal, 0.5 * lax.rsqrt(wave), 0.5)
+    slope = jnp.where(normal, 0.0, 0.25 / wave)
+    rows = jnp.broadcast_to(jnp.stack([shift * size, size, slope], axis=1)[:, :, None, :], (KX, 3, 8, LANES))
     lane = jnp.arange(LANES, dtype=jnp.int32)
-    part = jnp.arange(4, dtype=jnp.int32)
+    part = jnp.arange(2 * KX, dtype=jnp.int32)
     pick = (own[None, :, None] % SLOT == lane % SLOT) & (lane // SLOT == part[:, None, None])
+    pick = pick.reshape(2 * KX * LANES, LANES)
     flip = lane[:, None] + lane[None, :] == LANES - 1
     return by_degree, rows, pick.astype(jnp.bfloat16), flip.astype(jnp.bfloat16)
 
@@ -159,70 +168,89 @@
 
 def criterion_kernel(
     places, x_ref, hi_hbm, lo_hbm, degree_ref, rows_ref, pick_ref, flip_ref, out_ref,
-    hi_ref, lo_ref, xh_ref, xl_ref, low_ref, top_ref, sems,
+    hi_ref, lo_ref, xh_ref, xl_ref, low_ref, top_ref, vh_ref, vl_ref, res_ref, sems,
 ):
     copies = [
-        pltpu.make_async_copy(src.at[parity], dst.at[parity], sems.at[parity, k])
-        for parity in range(2)
-        for k, (src, dst) in enumerate(((hi_hbm, hi_ref), (lo_hbm, lo_ref)))
+        [
+            pltpu.make_async_copy(src.at[:, at, :], dst.at[:, at, :], sems.at[b, k])
+            for k, (src, dst) in enumerate(((hi_hbm, hi_ref), (lo_hbm, lo_ref)))
+        ]
+        for b, at in enumerate(pl.ds(start, BLOCK) for start in range(0, HALF, BLOCK))
     ]
-    for copy in copies:
+    for copy in sum(copies, []):
         copy.start()
     modes = x_ref.shape[0] // NY
     pair = 2 * NY // len(places)
-    sums = []
+    half = pair // 2
+    totals = [jnp.zeros((half, LANES), jnp.float32) for _ in range(2 * modes)]
     for parity in range(2):
         for m in range(modes):
             lanes = pl.ds(LANES * m, LANES)
-            total = jnp.zeros((pair // 2, LANES), jnp.float32)
-            shift = rows_ref[m, 0, :1]
-            for c in range(NY // pair):
-                at = pl.ds(c * pair // 2, pair // 2)
-                first = places[2 * c] * (pair // 2) * modes + parity * modes + m
-                x = x_ref[pl.ds(first, pair // 2, stride=2 * modes), :]
-                total = total + x * degree_ref[1, parity, at, :]
-                high, low = halves_of(x * (shift + degree_ref[0, parity, at, :]))
+            shift, size = rows_ref[m, 0, :1], rows_ref[m, 1, :1]
+            for row in range(0, HALF, half):
+                at = pl.ds(row, half)
+                first = places[2 * row // half] * half * modes + parity * modes + m
+                x = x_ref[pl.ds(first, half, stride=2 * modes), :]
+                totals[parity * modes + m] = totals[parity * modes + m] + x * degree_ref[1, parity, at, :]
+                high, low = halves_of(x * (shift + size * degree_ref[0, parity, at, :]))
                 xh_ref[parity, at, lanes] = high
                 xl_ref[parity, at, lanes] = low
-            sums.append(jnp.sum(total, axis=0, keepdims=True))
-    for copy in copies:
-        copy.wait()
-    halves = []
-    for parity in range(2):
-        xh = xh_ref[parity]
-        halves.append(
-            product(hi_ref[parity], xh) + product(hi_ref[parity], xl_ref[parity]) + product(lo_ref[parity], xh)
-        )
-    low_ref[pl.ds(8, HALF), :] = halves[0] + halves[1]
-    top_ref[pl.ds(8, HALF), :] = halves[0] - halves[1]
-    for m in range(modes):
-        lanes = pl.ds(LANES * m, LANES)
-        even, odd = sums[m], sums[modes + m]
-        low_ref[pl.ds(8, 1), lanes] = low_ref[pl.ds(8, 1), lanes] + (even + odd)
-        top_ref[pl.ds(8, 1), lanes] = top_ref[pl.ds(8, 1), lanes] + (even - odd)
     outside = jnp.zeros((8, LANES * modes), jnp.float32)
     low_ref[pl.ds(0, 8), :] = outside
     top_ref[pl.ds(0, 8), :] = outside
-    low_ref[pl.ds(8 + HALF, 1), :] = top_ref[pl.ds(7 + HALF, 1), :]
-    top_ref[pl.ds(8 + HALF, 1), :] = low_ref[pl.ds(7 + HALF, 1), :]
-    above = []
-    for b in range(HALF // LANES):
-        result = None
+
+    def values(start, size):
+        at = pl.ds(start, size)
         for part in range(2 * modes):
             ref, m = (low_ref, top_ref)[part // modes], part % modes
             lanes = pl.ds(LANES * m, LANES)
-            here = ref[pl.ds(8 + LANES * b, LANES), lanes]
-            slope = ref[pl.ds(9 + LANES * b, LANES), lanes] - ref[pl.ds(7 + LANES * b, LANES), lanes]
-            value = here * here * rows_ref[m, 1, :1] + slope * slope * rows_ref[m, 2, :1]
-            high, low = halves_of(value)
-            added = product(high, pick_ref[part]) + product(low, pick_ref[part])
-            result = added if result is None else result + added
-        turned = result.T
+            here = ref[pl.ds(8 + start, size), lanes]
+            slope = ref[pl.ds(9 + start, size), lanes] - ref[pl.ds(7 + start, size), lanes]
+            high, low = halves_of(here * here + slope * slope * rows_ref[m, 2, :1])
+            vh_ref[at, pl.ds(LANES * part, LANES)] = high
+            vl_ref[at, pl.ds(LANES * part, LANES)] = low
+        res_ref[at, :] = product(vh_ref[at, :], pick_ref[...]) + product(vl_ref[at, :], pick_ref[...])
+
+    done = 0
+    for start in range(0, HALF, BLOCK):
+        at = pl.ds(start, BLOCK)
+        for copy in copies[start // BLOCK]:
+            copy.wait()
+        halves = []
+        for parity in range(2):
+            xh = xh_ref[parity]
+            halves.append(
+                product(hi_ref[parity, at, :], xh) + product(hi_ref[parity, at, :], xl_ref[parity]) + product(lo_ref[parity, at, :], xh)
+            )
+        low_ref[pl.ds(8 + start, BLOCK), :] = halves[0] + halves[1]
+        top_ref[pl.ds(8 + start, BLOCK), :] = halves[0] - halves[1]
+        if start == 0:
+            for m in range(modes):
+                lanes = pl.ds(LANES * m, LANES)
+                even, odd = (
+                    rows_ref[m, 1, :1] * jnp.sum(totals[parity * modes + m], axis=0, keepdims=True) for parity in range(2)
+                )
+                low_ref[pl.ds(8, 1), lanes] = low_ref[pl.ds(8, 1), lanes] + (even + odd)
+                top_ref[pl.ds(8, 1), lanes] = top_ref[pl.ds(8, 1), lanes] + (even - odd)
+        if start + BLOCK == HALF:
+            low_ref[pl.ds(8 + HALF, 1), :] = top_ref[pl.ds(7 + HALF, 1), :]
+            top_ref[pl.ds(8 + HALF, 1), :] = low_ref[pl.ds(7 + HALF, 1), :]
+        ready = start + BLOCK if start + BLOCK == HALF else start + BLOCK - 8
+        while done < ready:
+            size = min(LANES, ready - done)
+            values(done, size)
+            done += size
+    above = []
+    for b in range(HALF // LANES):
+        turned = res_ref[pl.ds(LANES * b, LANES), :].T
         peer, at = divmod(LANES * b, out_ref.shape[-1])
         out_ref[peer, :, pl.ds(at, LANES)] = turned[: SLOT * modes]
-        high, low = halves_of(turned[SLOT * modes :])
+        above.append(turned[SLOT * modes :])
+    high, low = halves_of(jnp.concatenate(above, axis=0))
+    above = product(high, flip_ref[...]) + product(low, flip_ref[...])
+    for b in range(HALF // LANES):
         peer, at = divmod(NY - LANES * (b + 1), out_ref.shape[-1])
-        out_ref[peer, :, pl.ds(at, LANES)] = product(high, flip_ref[...]) + product(low, flip_ref[...])
+        out_ref[peer, :, pl.ds(at, LANES)] = above[SLOT * modes * b : SLOT * modes * (b + 1)]
 
 
 def criterion(field, high, low, numbers, places, peers):
@@ -236,7 +264,8 @@
         scratch_shapes=[pltpu.VMEM(high.shape, jnp.bfloat16)] * 2
         + [pltpu.VMEM((2, HALF, width), jnp.bfloat16)] * 2
         + [pltpu.VMEM((HALF + 16, width), jnp.float32)] * 2
-        + [pltpu.SemaphoreType.DMA((2, 2))],
+        + [pltpu.VMEM((HALF, 2 * width), jnp.bfloat16)] * 2
+        + [pltpu.VMEM((HALF, LANES), jnp.float32), pltpu.SemaphoreType.DMA((HALF // BLOCK, 2))],
         compiler_params=pltpu.CompilerParams(vmem_limit_bytes=LIMIT),
         name="criterion",
     )

time: 82.4 us -> 81 us (0.983)
  Pallas kernels: 11 us -> 9.62 us
    pallas_call x1, Pallas kernels: 6.52 us -> 5.33 us  [criterion(): return call(field.reshape(NY * modes, LANES), high, low, *numbers)]
where the time goes in v3:
time: 81 us; the launch traced here: 80.3 us
  waiting for transfers between devices  28.5 us (35%)
  blocking collectives  17.4 us (21%)
  starting transfers between devices  14.6 us (18%)
  Pallas kernels  9.62 us (12%)
  other arithmetic  6.04 us (7%)
  local copies, waits for them, and re-layouts  3.9 us (5%)
    all_to_all x1, waiting for transfers between devices, local(): field = lax.all_to_all(sent, ROUTE, split_axis=0, concat_axis=0, tiled=True)  28.5 us
    all_to_all x1, blocking collectives, local(): part = lax.all_to_all(part, 'gy', split_axis=0, concat_axis=0, tiled=True)  17.4 us
    all_to_all x1, starting transfers between devices, local(): field = lax.all_to_all(sent, ROUTE, split_axis=0, concat_axis=0, tiled=True)  14.6 us
    pallas_call x1, Pallas kernels, criterion(): return call(field.reshape(NY * modes, LANES), high, low, *numbers)  5.33 us
    unnamed x5, local copies, waits for them, and re-layouts  3.79 us
    cos x1, other arithmetic, tables(): jnp.cos(degrees)  2.78 us
    pallas_call x1, Pallas kernels, pack(): pl.pallas_call(lambda *refs: pack_kernel(places, span // peers, *refs), i...  2.71 us
  transfers between devices with their start and end apart: 1, of which 1 were waited for; matrix products, arithmetic and copies ran while one was open for 8% of the time, Pallas kernels for 2%

profile of v3, /device:TPU:6, one launch (start us, length us, event | category | flops | bytes accessed | tf_op | source)
XLA Modules:
  0.0 80.3 jit_solution(12348043412906429123)
XLA Ops:
  0.0 2.7 %pack.1 = f32[64,48,128]{2,1,0:T(8,128)} custom-call(f32[2,2,24,1920]{3,2,1,0:T(8,128)} %refs_0_.1, f32[2,2,24,1920]{3,2,1,0:T(8,128)} %refs_1_.1), custom_call_target="tpu_custom_call" | custom-call | tf_op jit(solution)/shard_map/pack/pallas_call | solution.py:91
  2.7 14.6 %all-to-all-start = ((f32[64,48,128]{2,1,0:T(8,128)}), f32[64,48,128]{2,1,0:T(8,128)S(1)}, u32[]{:S(2)}, u32[]{:S(2)}) async-start(f32[64,48,128]{2,1,0:T(8,128)} %pack.1), calls=%async_computation | async-start | bytes 3145728 | tf_op jit(solution)/shard_map/all_to_all | solution.py:281
  17.4 0.5 fusion.4
  17.9 2.8 %fusion.1 = (f32[2,1,768,128]{3,2,1,0:T(8,128)S(1)}, f32[2,1,768,128]{3,2,1,0:T(8,128)S(1)}) fusion(f32[1,1,768,128]{3,2,1,0:T(8,128)S(1)} %get-tuple-element.14, f32[1,1,768,128]{3,2,1,0:T(8,128)S(1)} %get-tuple-element.13), kind=kLoop, calls=%fused_computation.4 | loop fusion | flops 196608 | bytes 2359296 | tf_op jit(solution)/shard_map/cos | solution.py:129
  20.7 1.5 %fusion.9 = (f32[768,128]{1,0:T(8,128)S(1)}, f32[768,128]{1,0:T(8,128)S(1)}) fusion(s32[768]{0:T(1024)S(1)} %get-tuple-element.18, s32[768]{0:T(1024)S(1)} %get-tuple-element.19, pred[768]{0:T(1024)(128)(4,1)S(1)} %compare_and_fusion), kind=kLoop, calls=%fused_computation.15 | loop fusion | flops 294912 | bytes 793344 | tf_op jit(solution)/shard_map/cos | solution.py:129
  22.2 0.1 stack.33
  22.3 0.1 stack.32
  22.4 0.2 pad_maximum_fusion.base_ref
  22.6 1.6 %tables.1 = (bf16[2,768,768]{2,1,0:T(8,128)(2,1)S(1)}, bf16[2,768,768]{2,1,0:T(8,128)(2,1)S(1)}) custom-call(f32[2,4,768,128]{3,2,1,0:T(8,128)S(1)} %pad_maximum_fusion.base_ref), custom_call_target="tpu_custom_call" | custom-call | tf_op jit(solution)/shard_map/tables/pallas_call | solution.py:130
  24.2 0.0 copy-start
  24.2 1.4 %copy-done = bf16[2,768,768]{2,1,0:T(8,128)(2,1)} copy-done((bf16[2,768,768]{2,1,0:T(8,128)(2,1)}, bf16[2,768,768]{2,1,0:T(8,128)(2,1)S(1)}, u32[]{:S(2)}) %copy-start) | copy-done | bytes 2359320
  25.6 0.0 copy-start.1
  25.6 1.4 %copy-done.1 = bf16[2,768,768]{2,1,0:T(8,128)(2,1)} copy-done((bf16[2,768,768]{2,1,0:T(8,128)(2,1)}, bf16[2,768,768]{2,1,0:T(8,128)(2,1)S(1)}, u32[]{:S(2)}) %copy-start.1) | copy-done | bytes 2359320
  27.1 0.1 fusion.18
  27.2 0.2 sine_multiply_fusion
  27.4 0.1 broadcast_compare_fusion
  27.5 0.5 broadcast_select_fusion.refs_3_
  28.0 28.5 %all-to-all-done = f32[64,48,128]{2,1,0:T(8,128)S(1)} async-done(((f32[64,48,128]{2,1,0:T(8,128)}), f32[64,48,128]{2,1,0:T(8,128)S(1)}, u32[]{:S(2)}, u32[]{:S(2)}) %all-to-all-start) | async-done | bytes 1572896 | tf_op jit(solution)/shard_map/all_to_all | solution.py:281
  56.5 5.3 %criterion.1 = f32[4,64,384]{2,1,0:T(8,128)S(1)} custom-call(f32[3072,128]{1,0:T(8,128)S(1)} %bitcast.13, bf16[2,768,768]{2,1,0:T(8,128)(2,1)} %copy-done, bf16[2,768,768]{2,1,0:T(8,128)(2,1)} %copy-done.1, f32[2,2,768,128]{3,2,1,0:T(8,128)S(1)} %broadcast_select_fusion.refs_3_, f32[2,3,8,128]{3,2,1,0:T(8,128)S(1)} %broadcast_in_dim.60.refs_4_, ...), custom_call_target="tpu_custom_call" | custom-call | tf_op jit(solution)/shard_map/criterion/pallas_call | solution.py:273
  61.9 17.4 %all_to_all.10 = f32[4,64,384]{2,1,0:T(8,128)S(1)} all-to-all(f32[4,64,384]{2,1,0:T(8,128)S(1)} %criterion.1), channel_id=1, replica_groups=mesh['x'=4,'y'=4,'half'=2,'core'=2,'gy'=4] {'gy'}, dimensions={0} | all-to-all | bytes 786432 | tf_op jit(solution)/shard_map/all_to_all | solution.py:287
  79.3 1.0 %copy.6 = f32[4,2,30,384]{3,0,2,1:T(4,128)} copy(f32[4,2,30,384]{3,2,1,0:T(8,128)S(1)} %bitcast.15) | data formatting | bytes 737280
  (15 shorter events, 0.2 us)
Async XLA Ops:
  2.7 53.8 %all-to-all-start = ((f32[64,48,128]{2,1,0:T(8,128)}), f32[64,48,128]{2,1,0:T(8,128)S(1)}, u32[]{:S(2)}, u32[]{:S(2)}) async-start(f32[64,48,128]{2,1,0:T(8,128)} %pack.1), calls=%async_computation | async-start | bytes 3145728 | tf_op jit(solution)/shard_map/all_to_all | solution.py:281
  24.2 1.4 %copy-start = (bf16[2,768,768]{2,1,0:T(8,128)(2,1)}, bf16[2,768,768]{2,1,0:T(8,128)(2,1)S(1)}, u32[]{:S(2)}) copy-start(bf16[2,768,768]{2,1,0:T(8,128)(2,1)S(1)} %get-tuple-element.7.refs_1_) | copy-start | bytes 7077892
  25.6 1.4 %copy-start.1 = (bf16[2,768,768]{2,1,0:T(8,128)(2,1)}, bf16[2,768,768]{2,1,0:T(8,128)(2,1)S(1)}, u32[]{:S(2)}) copy-start(bf16[2,768,768]{2,1,0:T(8,128)(2,1)S(1)} %get-tuple-element.8.refs_2_) | copy-start | bytes 7077892
